TPU v7x, 512 devices: a whole 4x8x8 slice. The times are simulated.
512 devices in a mesh: blk: 64 (over z, y), head: 8 (over x, core).
Axes of the slice: x: 4, y: 8, z: 8, core: 2. Of those that a mesh axis runs over, the one named last changes fastest.
Arguments:
- tokens: bfloat16 [2048, 1024], P('blk'), may hold values from -6 to 6
- norm_gain: float32 [1024], replicated, may hold values from 0.25 to 1.75
- w_query: bfloat16 [1024, 1024], P(None, 'head')
- w_key: bfloat16 [1024, 1024], P(None, 'head'), may hold values from -0.1875 to 0.1875
- w_value: bfloat16 [1024, 1024], P(None, 'head'), may hold values from -0.1875 to 0.1875
- w_out: bfloat16 [1024, 1024], P('head'), may hold values from -0.1875 to 0.1875
- ffn_gain: float32 [1024], replicated, may hold values from 0.25 to 1.75
- w_gate: bfloat16 [1024, 4096], P(None, 'head'), may hold values from -0.1875 to 0.1875
- w_up: bfloat16 [1024, 4096], P(None, 'head'), may hold values from -0.1875 to 0.1875
- w_down: bfloat16 [4096, 1024], P('head'), may hold values from -0.09375 to 0.09375
- keys: bfloat16 [65536, 1024], P('blk', 'head'), may hold values from -6 to 6
- values: bfloat16 [65536, 1024], P('blk', 'head'), may hold values from -6 to 6
- key_variate: int32 [65536], P('blk'), may hold values from 0 to 3
- query_variate: int32 [2048], replicated, may hold values from 0 to 3
- bias: float32 [2, 16], P(None, 'head'), may hold values from -2 to 2
- lengths: int32 [2048], replicated, may hold values from 17 to 4096, as said below
- order: int32 [2048], replicated, may hold values from 0 to 2047, as said below
- live_blocks: int32 [1024], P('blk'), may hold values from 0 to 1
Outputs:
- layer_out: bfloat16 [2048, 1024], P('blk', 'head')
Inputs may be any that keep to these rules, and one draw needn't show every extreme that they name: lengths sum to 65536; the smallest is exactly 17 and the largest exactly 4096. Each request appears once; order[j] // 32 depends only on j % 64.
All inputs are finite; a program needn't handle non-finite values.
Results may differ from a plain program's by a relative error of at most 0.025.
Values may be sent and summed in bfloat16 or wider, within the bound.
A program may use at most 64 MiB of HBM per device.

v0:
```python
import jax
import jax.numpy as jnp
from jax import lax
from jax.sharding import PartitionSpec as P


def normalize(inputs, gain):
    mean_square = jnp.mean(inputs * inputs, axis=-1, keepdims=True)
    return inputs * lax.rsqrt(mean_square + 1e-05) * gain


def pool_owner(first, count, ends, order):
    position = first + jnp.arange(count, dtype=jnp.int32)
    rank = jnp.searchsorted(ends, position, side="right")
    return order[rank]


def key_scores(query_rows, key_rows, same, bias, head_dim):
    count = key_rows.shape[0]
    product = query_rows.astype(jnp.float32) * key_rows.astype(jnp.float32)
    raw = jnp.sum(product.reshape(count, -1, head_dim), axis=2) / jnp.sqrt(jnp.float32(head_dim))
    return raw + jnp.where(same[:, None], bias[0][None, :], bias[1][None, :])


def weighted_rows(weight, value_rows, head_dim):
    count = value_rows.shape[0]
    value_heads = value_rows.astype(jnp.float32).reshape(count, -1, head_dim)
    return (weight[:, :, None] * value_heads).reshape(count, -1)


def body(
    tokens,
    norm_gain,
    w_query,
    w_key,
    w_value,
    w_out,
    ffn_gain,
    w_gate,
    w_up,
    w_down,
    keys,
    values,
    key_variate,
    query_variate,
    bias,
    lengths,
    order,
    live_blocks,
):
    req_dev = tokens.shape[0]
    d_model = tokens.shape[1]
    heads_local = bias.shape[1]
    head_dim = w_query.shape[1] // heads_local
    pool_dev = keys.shape[0]
    block_len = pool_dev // live_blocks.shape[0]
    total_req = lengths.shape[0]
    here = lax.axis_index("blk")
    head_index = lax.axis_index("head")
    width_local = d_model // lax.axis_size("head")
    inputs = tokens.astype(jnp.float32)
    normed = normalize(inputs, norm_gain).astype(jnp.bfloat16)
    query = jnp.dot(normed, w_query, preferred_element_type=jnp.float32).astype(jnp.bfloat16)
    key_new = jnp.dot(normed, w_key, preferred_element_type=jnp.float32).astype(jnp.bfloat16)
    value_new = jnp.dot(normed, w_value, preferred_element_type=jnp.float32).astype(jnp.bfloat16)
    ends = jnp.cumsum(lengths[order])
    floor_value = jnp.float32(-1e30)
    live = jnp.repeat(live_blocks, block_len) > 0
    all_query = lax.all_gather(query, "blk", axis=0, tiled=True)
    owner = pool_owner(here * pool_dev, pool_dev, ends, order)
    same = key_variate == query_variate[owner]
    score = key_scores(all_query[owner], keys, same, bias, head_dim)
    masked = jnp.where(live[:, None], score, floor_value)
    local_top = jnp.full((total_req, heads_local), -1e30, jnp.float32).at[owner].max(masked)
    global_top = lax.pmax(local_top, "blk")
    weight = jnp.where(live[:, None], jnp.exp(masked - global_top[owner]), jnp.float32(0.0))
    value_part = jax.ops.segment_sum(
        weighted_rows(weight, values, head_dim), owner, num_segments=total_req
    )
    total_part = jax.ops.segment_sum(weight, owner, num_segments=total_req)
    value_sum, total_sum = (
        lax.psum_scatter(value_part, "blk", scatter_dimension=0, tiled=True),
        lax.psum_scatter(total_part, "blk", scatter_dimension=0, tiled=True),
    )
    run_top = lax.dynamic_slice_in_dim(global_top, here * req_dev, req_dev)
    query_heads = query.astype(jnp.float32).reshape(req_dev, heads_local, head_dim)
    own = (
        jnp.sum(
            query_heads * key_new.astype(jnp.float32).reshape(req_dev, heads_local, head_dim),
            axis=2,
        )
        / jnp.sqrt(jnp.float32(head_dim))
        + bias[0][None, :]
    )
    top_final = jnp.maximum(run_top, own)
    rescale = jnp.exp(run_top - top_final)
    own_weight = jnp.exp(own - top_final)
    total_final = total_sum * rescale + own_weight
    value_final = value_sum * jnp.repeat(rescale, head_dim, axis=1) + jnp.repeat(
        own_weight, head_dim, axis=1
    ) * value_new.astype(jnp.float32)
    attended = (value_final / jnp.repeat(total_final, head_dim, axis=1)).astype(jnp.bfloat16)
    projected = jnp.dot(attended, w_out, preferred_element_type=jnp.float32)
    head_part = lax.psum_scatter(
        projected.astype(jnp.bfloat16), "head", scatter_dimension=1, tiled=True
    ).astype(jnp.float32)
    input_slice = lax.dynamic_slice_in_dim(inputs, head_index * width_local, width_local, 1)
    mixed = (input_slice + head_part).astype(jnp.bfloat16)
    mixed_float = mixed.astype(jnp.float32)
    square_total = lax.psum(jnp.sum(mixed_float * mixed_float, axis=1), "head")
    gain_slice = lax.dynamic_slice_in_dim(ffn_gain, head_index * width_local, width_local)
    scaled = mixed_float * lax.rsqrt(square_total[:, None] / d_model + 1e-05) * gain_slice
    hidden_in = lax.all_gather(scaled.astype(jnp.bfloat16), "head", axis=1, tiled=True)
    gate = jnp.dot(hidden_in, w_gate, preferred_element_type=jnp.float32)
    upper = jnp.dot(hidden_in, w_up, preferred_element_type=jnp.float32)
    hidden = (jax.nn.silu(gate) * upper).astype(jnp.bfloat16)
    down_part = lax.psum_scatter(
        jnp.dot(hidden, w_down, preferred_element_type=jnp.float32).astype(jnp.bfloat16),
        "head",
        scatter_dimension=1,
        tiled=True,
    ).astype(jnp.float32)
    return (mixed_float + down_part).astype(jnp.bfloat16)


def solution(mesh):
    placed = (
        P("blk", None),
        P(),
        P(None, "head"),
        P(None, "head"),
        P(None, "head"),
        P("head", None),
        P(),
        P(None, "head"),
        P(None, "head"),
        P("head", None),
        P("blk", "head"),
        P("blk", "head"),
        P("blk"),
        P(),
        P(None, "head"),
        P(),
        P(),
        P("blk"),
    )
    return jax.shard_map(
        body, mesh=mesh, in_specs=placed, out_specs=P("blk", "head"), check_vma=False
    )
```

profile of v0, /device:TPU:1, one launch (start us, length us, event | category | flops | bytes accessed | tf_op | source)
XLA Modules:
  0.0 1064.1 jit_solution(11523997984311980912)
XLA Ops:
  7.3 11.8 %gather_fusion.1 = s32[2048]{0:T(1024)S(1)} fusion(s32[2048]{0:T(1024)S(1)} %copy-done.1, s32[2048]{0:T(1024)S(1)} %fusion.29), kind=kCustom, calls=%fused_computation.1 | custom fusion | bytes 24576 | tf_op jit(solution)/shard_map/gather | solution.py:66
  19.7 74.8 %while.24 = (s32[]{:T(128)}, u32[1024]{0:T(1024)S(1)}, u32[1024]{0:T(1024)S(1)}, s32[2048]{0:T(1024)S(1)}, s32[]{:T(128)}, /*index=5*/s32[]{:T(128)}, s32[]{:T(128)}, s32[]{}) while((s32[]{:T(128)}, u32[1024]{0:T(1024)S(1)}, u32[1024]{0:T(1024)S(1)}, s32[2048]{0:T(1024)S(1)}, s32[]{:T(128)}, /*index=5*/s32[]{:T(128)}, s32[]{:T(128)}, ...), condition=%wide.region_3.4_spmd.clone, body=%wide.region_2.3_spmd.clone.sunk | while | flops 20484 | bytes 63601 | solution.py:14
  19.7 6.2 gather_fusion
  26.0 6.2 gather_fusion
  32.2 6.2 gather_fusion
  38.4 6.2 gather_fusion
  44.7 6.2 gather_fusion
  50.9 6.2 gather_fusion
  57.2 6.2 gather_fusion
  63.4 6.2 gather_fusion
  69.6 6.2 gather_fusion
  75.9 6.2 gather_fusion
  82.1 6.2 gather_fusion
  88.4 6.2 gather_fusion
  95.3 6.1 gather_fusion.2
  102.4 45.7 %all_gather.6 = bf16[2048,128]{1,0:T(8,128)(2,1)S(1)} all-gather(bf16[32,128]{1,0:T(8,128)(2,1)S(1)} %convolution_convert_fusion.4), channel_id=1, replica_groups=mesh['blk'=64,'head'=8] {'blk'}, dimensions={0}, use_global_device_ids=true | all-gather | bytes 532480 | tf_op jit(solution)/shard_map/all_gather | solution.py:69
  148.1 3.2 gather_fusion.3
  152.3 6.1 gather_fusion.4
  160.1 7.7 scatter_custom_fusion
  167.8 230.1 %pmax.7 = f32[2048,2]{1,0:T(8,128)S(1)} all-reduce(f32[2048,2]{1,0:T(8,128)S(1)} %scatter_custom_fusion), channel_id=1, replica_groups=mesh['blk'=64,'head'=8] {'blk'}, use_global_device_ids=true, to_apply=%region_7.8 | all-reduce | flops 4096 | bytes 32768 | tf_op jit(solution)/shard_map/pmax | solution.py:75
  398.0 2.8 gather_fusion.5
  401.3 8.5 scatter_custom_fusion.2
  409.9 0.9 copy-done.7
  411.2 8.5 scatter_custom_fusion.1
  419.8 0.9 copy-done.8
  421.1 287.2 %reduce-scatter.11.cloned.1.call-done = f32[32,2]{1,0:T(8,128)} async-done(((f32[2048,2]{1,0:T(8,128)}), f32[32,2]{1,0:T(8,128)}) %reduce-scatter.11.cloned.1.call-update) | async-done | bytes 272 | tf_op jit(solution)/shard_map/reduce_scatter | solution.py:83
  709.6 244.1 %reduce-scatter.9.cloned.1.call-done = f32[32,128]{1,0:T(8,128)} async-done(((f32[2048,128]{1,0:T(8,128)}), f32[32,128]{1,0:T(8,128)}) %reduce-scatter.9.cloned.1.call-update) | async-done | bytes 16400 | tf_op jit(solution)/shard_map/reduce_scatter | solution.py:82
  953.7 1.3 convolution_convert_fusion.1
  956.8 35.8 %reduce-scatter.13.cloned.1.call-done = bf16[128,32]{1,0:T(8,128)(2,1)} async-done(((bf16[1024,32]{1,0:T(8,128)(2,1)}), bf16[128,32]{1,0:T(8,128)(2,1)}) %reduce-scatter.13.cloned.1.call-update) | async-done | bytes 8208
  993.5 14.0 %psum.7 = f32[32]{0:T(128)S(1)} all-reduce(f32[32]{0:T(128)S(1)} %get-tuple-element.104), channel_id=1, replica_groups=mesh['blk'=64,'head'=8] {'head'}, use_global_device_ids=true, to_apply=%region_15.16 | all-reduce | flops 32 | bytes 256 | tf_op jit(solution)/shard_map/psum | solution.py:110
  1007.6 13.1 %all_gather.7 = bf16[32,1024]{1,0:T(8,128)(2,1)S(1)} all-gather(bf16[32,128]{1,0:T(8,128)(2,1)S(1)} %fusion.26), channel_id=1, replica_groups=mesh['blk'=64,'head'=8] {'head'}, dimensions={1}, use_global_device_ids=true | all-gather | bytes 73728 | tf_op jit(solution)/shard_map/all_gather | solution.py:113
  1022.4 33.7 %reduce-scatter.15.cloned.1.call-done = bf16[128,32]{1,0:T(8,128)(2,1)} async-done(((bf16[1024,32]{1,0:T(8,128)(2,1)}), bf16[128,32]{1,0:T(8,128)(2,1)}) %reduce-scatter.15.cloned.1.call-update) | async-done | bytes 8208
  (142 shorter events, 14.5 us)
Async XLA Ops:
  6.5 1014.4 %copy-start = (bf16[512,1024]{1,0:T(8,128)(2,1)S(1)}, bf16[512,1024]{1,0:T(8,128)(2,1)}, u32[]{:S(2)}) copy-start(bf16[512,1024]{1,0:T(8,128)(2,1)} %param.29) | copy-start | bytes 3145732
  6.5 701.8 %reduce-scatter.11.cloned.1.call-start = ((), (), s32[]{:S(2)}) async-start(), calls=%async_computation.5 | async-start | bytes 1064960 | tf_op jit(solution)/shard_map/reduce_scatter | solution.py:83
  6.5 0.8 copy-start.1
  94.6 0.7 copy-start.2
  95.3 6.2 copy-start.5
  95.3 6.3 copy-start.16
  101.5 0.7 copy-start.11
  102.2 317.7 %copy-start.14 = (f32[32]{0:T(128)}, f32[32]{0:T(128)S(1)}, u32[]{:S(2)}) copy-start(f32[32]{0:T(128)S(1)} %add_rsqrt_fusion.1) | copy-start | bytes 388
  148.1 3.2 copy-start.10
  151.6 0.7 copy-start.3
  152.3 6.2 copy-start.15
  158.4 0.7 copy-start.17
  159.1 241.9 %copy-start.12 = (f32[2]{0:T(128)}, f32[2]{0:T(128)S(1)}, u32[]{:S(2)}) copy-start(f32[2]{0:T(128)S(1)} %get-tuple-element.109) | copy-start | bytes 28
  159.1 0.7 copy-start.13
  409.8 0.9 copy-start.7
  409.9 543.9 %reduce-scatter.9.cloned.1.call-start = ((), (), s32[]{:S(2)}) async-start(), calls=%async_computation.4 | async-start | bytes 1064960 | tf_op jit(solution)/shard_map/reduce_scatter | solution.py:82
  419.7 0.9 copy-start.8
  419.8 572.8 %reduce-scatter.13.cloned.1.call-start = ((), (), s32[]{:S(2)}) async-start(), calls=%async_computation.6 | async-start | bytes 294912
  420.9 532.8 %copy-start.9 = (bf16[128,1024]{1,0:T(8,128)(2,1)S(1)}, bf16[128,1024]{1,0:T(8,128)(2,1)}, u32[]{:S(2)}) copy-start(bf16[128,1024]{1,0:T(8,128)(2,1)} %param.25) | copy-start | bytes 786436
  421.1 599.6 %copy-start.4 = (bf16[1024,512]{1,0:T(8,128)(2,1)S(1)}, bf16[1024,512]{1,0:T(8,128)(2,1)}, u32[]{:S(2)}) copy-start(bf16[1024,512]{1,0:T(8,128)(2,1)} %param.27) | copy-start | bytes 3145732
  955.0 65.9 %copy-start.6 = (bf16[1024,512]{1,0:T(8,128)(2,1)S(1)}, bf16[1024,512]{1,0:T(8,128)(2,1)}, u32[]{:S(2)}) copy-start(bf16[1024,512]{1,0:T(8,128)(2,1)} %param.28) | copy-start | bytes 3145732
  955.9 100.2 %reduce-scatter.15.cloned.1.call-start = ((), (), s32[]{:S(2)}) async-start(), calls=%async_computation.7 | async-start | bytes 294912
Sparse Core Ops, SparseCore 0:
  410.0 298.2 reduce-scatter.10
  712.9 240.7 reduce-scatter.8
  956.5 36.0 reduce-scatter.12
  1022.5 33.5 reduce-scatter.14
where the time goes:
time: 1070 us; the launch traced here: 1060 us
  waiting for transfers between devices  601 us (56%)
  blocking collectives  303 us (28%)
  local copies, waits for them, and re-layouts  115 us (11%)
  other arithmetic  28.5 us (3%)
  between operations  13.5 us (1%)
    reduce_scatter x1, waiting for transfers between devices, body(): lax.psum_scatter(total_part, 'blk', scatter_dimension=0, tiled=True)  287 us
    reduce_scatter x1, waiting for transfers between devices, body(): lax.psum_scatter(value_part, 'blk', scatter_dimension=0, tiled=True)  244 us
    pmax x1, blocking collectives, body(): global_top = lax.pmax(local_top, 'blk')  230 us
    gather x12, local copies, waits for them, and re-layouts, pool_owner(): rank = jnp.searchsorted(ends, position, side='right')  73.8 us
    unnamed x6, waiting for transfers between devices  69.6 us
    all_gather x1, blocking collectives, body(): all_query = lax.all_gather(query, 'blk', axis=0, tiled=True)  45.7 us
  transfers between devices with their start and end apart: 4, of which 4 were waited for; matrix products, arithmetic and copies ran while one was open for 1% of the time, Pallas kernels for 0%

commit v1 on v0

v1 whole, which is shorter than its diff:
```python
import functools

import jax
import jax.numpy as jnp
from jax import lax
from jax.experimental import pallas as pl
from jax.experimental.pallas import tpu as pltpu
from jax.sharding import PartitionSpec as P

F32 = jnp.float32
BF16 = jnp.bfloat16
HIGH = lax.Precision.HIGHEST
FLOOR = -1e30


def iota(shape, dim):
    return lax.broadcasted_iota(jnp.int32, shape, dim)


def dot(a, b):
    return jnp.dot(a, b, preferred_element_type=F32)


def dot_nt(a, b, precision=None):
    return lax.dot_general(
        a, b, (((1,), (1,)), ((), ())), preferred_element_type=F32, precision=precision
    )


def dot_tn(a, b, precision=None):
    return lax.dot_general(
        a, b, (((0,), (0,)), ((), ())), preferred_element_type=F32, precision=precision
    )


def row_dot(a, b):
    return jnp.dot(a, b, preferred_element_type=F32, precision=HIGH)


def kernel(
    tok_ref,
    norm_gain_ref,
    ffn_gain_ref,
    order_ref,
    len_ref,
    query_variate_ref,
    key_variate_ref,
    live_ref,
    bias_ref,
    wq_hbm,
    wk_hbm,
    wv_hbm,
    keys_hbm,
    values_hbm,
    wo_hbm,
    wg_hbm,
    wu_hbm,
    wd_hbm,
    out_ref,
    wq,
    wk,
    wv,
    keys,
    values,
    wo,
    wg,
    wu,
    wd,
    q_send,
    q_recv,
    p_send,
    p_recv,
    c_send,
    c_recv,
    d_recv,
    e_send,
    e_recv,
    load_sem,
    send_sem,
    recv_sem,
):
    n_blk = q_send.shape[0]
    n_head = c_send.shape[0]
    reqs, d_model = tok_ref.shape
    pool = keys.shape[0]
    n_live = live_ref.shape[1]
    block = pool // n_live
    width = c_send.shape[2]
    half = width // 2
    me = lax.axis_index("blk")
    head = lax.axis_index("head")

    loads = []
    for at, (src, dst) in enumerate(
        (
            (wq_hbm, wq),
            (wk_hbm, wk),
            (wv_hbm, wv),
            (keys_hbm, keys),
            (values_hbm, values),
            (wo_hbm, wo),
            (wg_hbm, wg),
            (wu_hbm, wu),
            (wd_hbm, wd),
        )
    ):
        copy = pltpu.make_async_copy(src, dst, load_sem.at[at])
        copy.start()
        loads.append(copy)

    barrier = pltpu.get_barrier_semaphore()

    def greet_blk(i, carry):
        pl.semaphore_signal(barrier, inc=1, device_id={"blk": lax.rem(me + i, n_blk)})
        return carry

    def greet_head(i, carry):
        pl.semaphore_signal(barrier, inc=1, device_id={"head": lax.rem(head + i, n_head)})
        return carry

    lax.fori_loop(1, n_blk, greet_blk, 0)
    lax.fori_loop(1, n_head, greet_head, 0)

    order = order_ref[...]
    rows, lanes = order.shape
    home = order[0:1, :] >> 5
    local = order & (reqs - 1)
    packed = (len_ref[...] + (query_variate_ref[...] << 13)).astype(F32)
    per_row = lanes // reqs
    table = jnp.zeros((reqs, lanes), F32)
    for part in range(per_row):
        pick = (home == iota((rows, lanes), 0) * per_row + part).astype(F32)
        found = dot_tn(packed, pick, HIGH)
        table = table + found[part * reqs : (part + 1) * reqs, :]
    ordered = jnp.zeros((rows, lanes), F32)
    for slot in range(reqs):
        ordered = ordered + jnp.where(local == slot, table[slot : slot + 1, :], 0.0)
    ordered = ordered.astype(jnp.int32)
    variate = (ordered >> 13).astype(F32)
    length = (ordered & 8191).astype(F32)
    upper = (iota((lanes, lanes), 0) <= iota((lanes, lanes), 1)).astype(F32)
    prefix = row_dot(length, upper)
    below = (iota((rows, rows), 1) < iota((rows, rows), 0)).astype(F32)
    totals = jnp.broadcast_to(jnp.sum(length, axis=1, keepdims=True), (rows, lanes))
    ends = prefix + row_dot(below, totals)
    starts = ends - length

    mine = jnp.where(home == me, local, -1)
    start_acc = jnp.zeros((reqs, lanes), F32)
    end_acc = jnp.zeros((reqs, lanes), F32)
    slot_id = iota((reqs, lanes), 0)
    for row in range(rows):
        hit = mine[row : row + 1, :] == slot_id
        start_acc = start_acc + jnp.where(hit, starts[row : row + 1, :], 0.0)
        end_acc = end_acc + jnp.where(hit, ends[row : row + 1, :], 0.0)
    start_req = jnp.sum(start_acc, axis=1, keepdims=True)
    end_req = jnp.sum(end_acc, axis=1, keepdims=True)
    first = (iota((reqs, n_blk), 1) * pool).astype(F32)
    holds = (end_req > first) & (start_req < first + pool)
    holds_f = holds.astype(F32)

    inputs = tok_ref[...].astype(F32)
    mean_square = jnp.mean(inputs * inputs, axis=1, keepdims=True)
    normed = (inputs * lax.rsqrt(mean_square + 1e-05) * norm_gain_ref[...]).astype(BF16)
    loads[0].wait()
    query = dot(normed, wq[...]).astype(BF16)
    query_f = query.astype(F32)
    routed = dot_tn(holds_f.astype(BF16), query)
    q_send[...] = routed.reshape(n_blk, 1, width)
    q_recv[pl.ds(me, 1)] = q_send[pl.ds(me, 1)]

    pl.semaphore_wait(barrier, n_blk + n_head - 2)

    def exchange_blk(send, recv, at):
        def step(i, carry):
            to = lax.rem(me + i, n_blk)
            pltpu.make_async_remote_copy(
                src_ref=send.at[to],
                dst_ref=recv.at[me],
                send_sem=send_sem.at[at],
                recv_sem=recv_sem.at[at],
                device_id={"blk": to},
            ).start()
            return carry

        lax.fori_loop(1, n_blk, step, 0)

    def exchange_head(send, recv, at):
        def step(i, carry):
            to = lax.rem(head + i, n_head)
            pltpu.make_async_remote_copy(
                src_ref=send(to),
                dst_ref=recv.at[head],
                send_sem=send_sem.at[at],
                recv_sem=recv_sem.at[at],
                device_id={"head": to},
            ).start()
            return carry

        lax.fori_loop(1, n_head, step, 0)

    def wait_bytes(ref, sem, at):
        part = ref.at[pl.ds(0, ref.shape[0] - 1)]
        pltpu.make_async_copy(part, part, sem.at[at]).wait()

    exchange_blk(q_send, q_recv, 0)

    loads[1].wait()
    key_new = dot(normed, wk[...]).astype(BF16).astype(F32)
    loads[2].wait()
    value_new = dot(normed, wv[...]).astype(BF16).astype(F32)
    product = query_f * key_new
    left = iota((reqs, width), 1) < half
    scale = 1.0 / (half**0.5)
    own = [
        jnp.sum(jnp.where(left, product, 0.0), axis=1, keepdims=True) * scale + bias_ref[0, 0],
        jnp.sum(jnp.where(left, 0.0, product), axis=1, keepdims=True) * scale + bias_ref[0, 1],
    ]
    base = (me * pool).astype(F32)
    meets = (ends > base) & (starts < base + pool)
    start_lane = jnp.sum(jnp.where(meets, starts - base, 0.0), axis=0, keepdims=True)
    end_lane = jnp.sum(jnp.where(meets, ends - base, 0.0), axis=0, keepdims=True)
    variate_lane = jnp.sum(jnp.where(meets, variate, 0.0), axis=0, keepdims=True)
    at_home = home == iota((n_blk, lanes), 0)
    start_slot = jnp.sum(jnp.where(at_home, start_lane, 0.0), axis=1, keepdims=True)
    end_slot = jnp.sum(jnp.where(at_home, end_lane, 0.0), axis=1, keepdims=True)
    variate_slot = jnp.sum(jnp.where(at_home, variate_lane, 0.0), axis=1, keepdims=True)
    in_block = (iota((n_live, pool), 1) // block == iota((n_live, pool), 0)).astype(BF16)
    live = dot(jnp.broadcast_to(live_ref[...].astype(F32).astype(BF16), (8, n_live)), in_block)[0:1, :]
    token = iota((n_blk, pool), 1).astype(F32)
    mask = (token >= start_slot) & (token < end_slot) & (live > 0.5)
    same = key_variate_ref[...].astype(F32) == variate_slot
    loads[3].wait()
    loads[4].wait()

    wait_bytes(q_recv, recv_sem, 0)
    queries = q_recv[...].reshape(n_blk, width)
    left_slot = iota((n_blk, width), 1) < half
    stacked = jnp.concatenate(
        [jnp.where(left_slot, queries, 0.0), jnp.where(left_slot, 0.0, queries)], axis=0
    ).astype(BF16)
    raw = dot_nt(stacked, keys[...])
    tops, sums, weights = [], [], []
    for at in range(2):
        score = raw[at * n_blk : (at + 1) * n_blk, :] * scale + jnp.where(
            same, bias_ref[0, at], bias_ref[1, at]
        )
        top = jnp.max(jnp.where(mask, score, FLOOR), axis=1, keepdims=True)
        weight = jnp.where(mask, jnp.exp(score - top), 0.0)
        tops.append(top)
        sums.append(jnp.sum(weight, axis=1, keepdims=True))
        weights.append(weight.astype(BF16))
    summed = dot(jnp.concatenate(weights, axis=0), values[...])
    summed = jnp.where(left_slot, summed[:n_blk, :], summed[n_blk:, :])
    column = iota((n_blk, width), 1)
    stats = jnp.where(
        column < 1,
        tops[0],
        jnp.where(column < 2, tops[1], jnp.where(column < 3, sums[0], sums[1])),
    )
    p_send[:, 0:1, :] = summed.reshape(n_blk, 1, width)
    p_send[:, 1:2, :] = stats.reshape(n_blk, 1, width)
    p_recv[pl.ds(me, 1)] = p_send[pl.ds(me, 1)]
    exchange_blk(p_send, p_recv, 1)
    wait_bytes(p_recv, recv_sem, 1)

    part_sum = p_recv[:, 0:1, :].reshape(n_blk, width)
    part_stat = p_recv[:, 1:2, :].reshape(n_blk, width)
    choose = (iota((8, width), 0) == iota((8, width), 1)).astype(F32)
    by_lane = dot_nt(choose, part_stat, HIGH)
    merged, total = [], []
    own_weight = []
    for at in range(2):
        part_top = by_lane[at : at + 1, :]
        part_total = by_lane[2 + at : 3 + at, :]
        top = jnp.maximum(
            own[at], jnp.max(jnp.where(holds, part_top, FLOOR), axis=1, keepdims=True)
        )
        factor = jnp.where(holds, jnp.exp(part_top - top), 0.0)
        mine_weight = jnp.exp(own[at] - top)
        total.append(jnp.sum(factor * part_total, axis=1, keepdims=True) + mine_weight)
        own_weight.append(mine_weight)
        merged.append(row_dot(factor, part_sum))
    value_final = jnp.where(left, merged[0], merged[1]) + jnp.where(
        left, own_weight[0], own_weight[1]
    ) * value_new
    attended = (value_final / jnp.where(left, total[0], total[1])).astype(BF16)
    loads[5].wait()
    projected = dot(attended, wo[...]).astype(BF16)
    for at in range(n_head):
        c_send[at] = projected[:, at * width : (at + 1) * width]
    c_recv[pl.ds(head, 1)] = c_send[pl.ds(head, 1)]
    exchange_head(lambda to: c_send.at[to], c_recv, 2)
    wait_bytes(c_recv, recv_sem, 2)
    mixed = tok_ref[:, pl.ds(pl.multiple_of(head * width, width), width)].astype(F32)
    part = c_recv[0].astype(F32)
    for at in range(1, n_head):
        part = part + c_recv[at].astype(F32)
    mixed = (mixed + part).astype(BF16)
    d_recv[pl.ds(head, 1)] = mixed.reshape(1, reqs, width)
    exchange_head(lambda to: d_recv.at[head], d_recv, 3)
    wait_bytes(d_recv, recv_sem, 3)
    square = jnp.zeros((reqs, width), F32)
    gathered = []
    for at in range(n_head):
        piece = d_recv[at].astype(F32)
        gathered.append(piece)
        square = square + piece * piece
    inverse = lax.rsqrt(jnp.sum(square, axis=1, keepdims=True) / d_model + 1e-05)
    hidden_in = jnp.concatenate(
        [
            (gathered[at] * inverse * ffn_gain_ref[:, at * width : (at + 1) * width]).astype(BF16)
            for at in range(n_head)
        ],
        axis=1,
    )
    loads[6].wait()
    gate = dot(hidden_in, wg[...])
    loads[7].wait()
    upper_units = dot(hidden_in, wu[...])
    hidden = (gate * jax.nn.sigmoid(gate) * upper_units).astype(BF16)
    loads[8].wait()
    down = dot(hidden, wd[...]).astype(BF16)
    for at in range(n_head):
        e_send[at] = down[:, at * width : (at + 1) * width]
    e_recv[pl.ds(head, 1)] = e_send[pl.ds(head, 1)]
    exchange_head(lambda to: e_send.at[to], e_recv, 4)
    wait_bytes(e_recv, recv_sem, 4)
    part = e_recv[0].astype(F32)
    for at in range(1, n_head):
        part = part + e_recv[at].astype(F32)
    out_ref[...] = (mixed.astype(F32) + part).astype(BF16)
    wait_bytes(q_send, send_sem, 0)
    wait_bytes(p_send, send_sem, 1)
    wait_bytes(c_send, send_sem, 2)
    wait_bytes(d_recv, send_sem, 3)
    wait_bytes(e_send, send_sem, 4)


def body(
    tokens,
    norm_gain,
    w_query,
    w_key,
    w_value,
    w_out,
    ffn_gain,
    w_gate,
    w_up,
    w_down,
    keys,
    values,
    key_variate,
    query_variate,
    bias,
    lengths,
    order,
    live_blocks,
):
    n_blk = lax.axis_size("blk")
    n_head = lax.axis_size("head")
    reqs, d_model = tokens.shape
    width = d_model // n_head
    vmem = pl.BlockSpec(memory_space=pltpu.VMEM)
    smem = pl.BlockSpec(memory_space=pltpu.SMEM)
    hbm = pl.BlockSpec(memory_space=pl.ANY)
    big = (w_query, w_key, w_value, keys, values, w_out, w_gate, w_up, w_down)
    return pl.pallas_call(
        kernel,
        out_shape=jax.ShapeDtypeStruct((reqs, width), BF16),
        in_specs=[vmem] * 8 + [smem] + [hbm] * len(big),
        out_specs=vmem,
        scratch_shapes=[pltpu.VMEM(x.shape, x.dtype) for x in big]
        + [
            pltpu.VMEM((n_blk, 1, width), F32),
            pltpu.VMEM((n_blk, 1, width), F32),
            pltpu.VMEM((n_blk, 2, width), F32),
            pltpu.VMEM((n_blk, 2, width), F32),
        ]
        + [pltpu.VMEM((n_head, reqs, width), BF16)] * 5
        + [
            pltpu.SemaphoreType.DMA((len(big),)),
            pltpu.SemaphoreType.DMA((5,)),
            pltpu.SemaphoreType.DMA((5,)),
        ],
        compiler_params=pltpu.CompilerParams(
            collective_id=0, has_side_effects=True, vmem_limit_bytes=40 * 1024 * 1024
        ),
    )(
        tokens,
        norm_gain.reshape(1, -1),
        ffn_gain.reshape(1, -1),
        order.reshape(-1, 128),
        lengths.reshape(-1, 128),
        query_variate.reshape(-1, 128),
        key_variate.reshape(1, -1),
        live_blocks.reshape(1, -1),
        bias,
        *big,
    )


def solution(mesh):
    placed = (
        P("blk", None),
        P(),
        P(None, "head"),
        P(None, "head"),
        P(None, "head"),
        P("head", None),
        P(),
        P(None, "head"),
        P(None, "head"),
        P("head", None),
        P("blk", "head"),
        P("blk", "head"),
        P("blk"),
        P(),
        P(None, "head"),
        P(),
        P(),
        P("blk"),
    )
    return jax.shard_map(
        body, mesh=mesh, in_specs=placed, out_specs=P("blk", "head"), check_vma=False
    )
```

time: 1070 us -> 61.7 us (0.06)
  waiting for transfers between devices: 601 us -> 0 us
  blocking collectives: 303 us -> 0 us
  local copies, waits for them, and re-layouts: 115 us -> 14.9 us
  Pallas kernels: 0 us -> 46.1 us
  other arithmetic: 28.5 us -> 0 us
  between operations: 13.5 us -> 0.03 us
    reduce_scatter x2 -> x0, waiting for transfers between devices: 531 us -> none  [the longest x1 287 us: body(): lax.psum_scatter(total_part, 'blk', scatter_dimension=0, tiled=True)]
    pmax x1 -> x0, blocking collectives: 230 us -> none  [body(): global_top = lax.pmax(local_top, 'blk')]
    gather x18 -> x0, local copies, waits for them, and re-layouts: 104 us -> none  [the longest x12 73.8 us: pool_owner(): rank = jnp.searchsorted(ends, position, side='right')]
    unnamed x6 -> x0, waiting for transfers between devices: 69.6 us -> none
    all_gather x2 -> x0, blocking collectives: 58.8 us -> none  [the longest x1 45.7 us: body(): all_query = lax.all_gather(query, 'blk', axis=0, tiled=True)]
    pallas_call x0 -> x1, Pallas kernels: none -> 46.1 us  [body(): pl.pallas_call(kernel, out_shape=jax.ShapeDtypeStruct((reqs, width), BF16...]
    scatter-add x2 -> x0, other arithmetic: 17.1 us -> none  [the longest x1 8.55 us: body(): jax.ops.segment_sum(weighted_rows(weight, values, head_dim), owner, num_s...]
    psum x1 -> x0, blocking collectives: 14 us -> none  [body(): square_total = lax.psum(jnp.sum(mixed_float * mixed_float, axis=1), 'head')]
  transfers between devices with their start and end apart: 4 -> 0, of which waited for: 4 -> 0; matrix products, arithmetic and copies ran while one was open for 1% -> 0% of each run, Pallas kernels for 0% -> 0%
where the time goes in v1:
time: 61.7 us; the launch traced here: 61.1 us
  Pallas kernels  46.1 us (75%)
  local copies, waits for them, and re-layouts  14.9 us (24%)
    pallas_call x1, Pallas kernels, body(): pl.pallas_call(kernel, out_shape=jax.ShapeDtypeStruct((reqs, width), BF16...  46.1 us
    unnamed x37, local copies, waits for them, and re-layouts  14.9 us

profile of v1, /device:TPU:1, one launch (start us, length us, event | category | flops | bytes accessed | tf_op | source)
XLA Modules:
  0.0 61.1 jit_solution(2659440511936163789)
XLA Ops:
  0.0 0.0 copy-start.10
  0.0 0.0 copy-start.13
  0.0 0.0 copy-start.16
  0.0 0.7 %copy-done.10 = s32[2048]{0:T(1024)S(1)} copy-done((s32[2048]{0:T(1024)S(1)}, s32[2048]{0:T(1024)}, u32[]{:S(2)}) %copy-start.10) | copy-done | bytes 8216
  0.7 0.0 copy-done.13
  0.7 0.0 copy-done.16
  0.7 0.0 copy-start
  0.7 1.2 %copy-done = bf16[1024,512]{1,0:T(8,128)(2,1)S(1)} copy-done((bf16[1024,512]{1,0:T(8,128)(2,1)S(1)}, bf16[1024,512]{1,0:T(8,128)(2,1)}, u32[]{:S(2)}) %copy-start) | copy-done | bytes 1048600
  1.9 0.0 copy-start.1
  1.9 1.2 %copy-done.1 = bf16[1024,512]{1,0:T(8,128)(2,1)S(1)} copy-done((bf16[1024,512]{1,0:T(8,128)(2,1)S(1)}, bf16[1024,512]{1,0:T(8,128)(2,1)}, u32[]{:S(2)}) %copy-start.1) | copy-done | bytes 1048600
  3.2 0.0 copy-start.2
  3.2 1.2 %copy-done.2 = bf16[512,1024]{1,0:T(8,128)(2,1)S(1)} copy-done((bf16[512,1024]{1,0:T(8,128)(2,1)S(1)}, bf16[512,1024]{1,0:T(8,128)(2,1)}, u32[]{:S(2)}) %copy-start.2) | copy-done | bytes 1048600
  4.4 0.0 copy-start.3
  4.4 0.9 %copy-done.3 = bf16[1024,128]{1,0:T(8,128)(2,1)S(1)} copy-done((bf16[1024,128]{1,0:T(8,128)(2,1)S(1)}, bf16[1024,128]{1,0:T(8,128)(2,1)}, u32[]{:S(2)}) %copy-start.3) | copy-done | bytes 262168
  5.3 0.0 copy-start.4
  5.3 0.9 %copy-done.4 = bf16[1024,128]{1,0:T(8,128)(2,1)S(1)} copy-done((bf16[1024,128]{1,0:T(8,128)(2,1)S(1)}, bf16[1024,128]{1,0:T(8,128)(2,1)}, u32[]{:S(2)}) %copy-start.4) | copy-done | bytes 262168
  6.3 0.0 copy-start.5
  6.3 0.9 %copy-done.5 = bf16[1024,128]{1,0:T(8,128)(2,1)S(1)} copy-done((bf16[1024,128]{1,0:T(8,128)(2,1)S(1)}, bf16[1024,128]{1,0:T(8,128)(2,1)}, u32[]{:S(2)}) %copy-start.5) | copy-done | bytes 262168
  7.2 0.9 %copy-done.6 = bf16[1024,128]{1,0:T(8,128)(2,1)S(1)} copy-done((bf16[1024,128]{1,0:T(8,128)(2,1)S(1)}, bf16[1024,128]{1,0:T(8,128)(2,1)}, u32[]{:S(2)}) %copy-start.6) | copy-done | bytes 262168
  8.2 0.0 copy-start.7
  8.2 0.9 %copy-done.7 = bf16[1024,128]{1,0:T(8,128)(2,1)S(1)} copy-done((bf16[1024,128]{1,0:T(8,128)(2,1)S(1)}, bf16[1024,128]{1,0:T(8,128)(2,1)}, u32[]{:S(2)}) %copy-start.7) | copy-done | bytes 262168
  9.1 0.0 copy-start.8
  9.1 0.9 %copy-done.8 = bf16[128,1024]{1,0:T(8,128)(2,1)S(1)} copy-done((bf16[128,1024]{1,0:T(8,128)(2,1)S(1)}, bf16[128,1024]{1,0:T(8,128)(2,1)}, u32[]{:S(2)}) %copy-start.8) | copy-done | bytes 262168
  10.1 0.0 copy-start.9
  10.1 0.8 %copy-done.9 = bf16[32,1024]{1,0:T(8,128)(2,1)S(1)} copy-done((bf16[32,1024]{1,0:T(8,128)(2,1)S(1)}, bf16[32,1024]{1,0:T(8,128)(2,1)}, u32[]{:S(2)}) %copy-start.9) | copy-done | bytes 65560
  10.9 0.7 %copy-done.11 = s32[2048]{0:T(1024)S(1)} copy-done((s32[2048]{0:T(1024)S(1)}, s32[2048]{0:T(1024)}, u32[]{:S(2)}) %copy-start.11) | copy-done | bytes 8216
  11.6 0.7 %copy-done.12 = s32[2048]{0:T(1024)S(1)} copy-done((s32[2048]{0:T(1024)S(1)}, s32[2048]{0:T(1024)}, u32[]{:S(2)}) %copy-start.12) | copy-done | bytes 8216
  12.3 0.7 %copy-done.14 = f32[1024]{0:T(1024)S(1)} copy-done((f32[1024]{0:T(1024)S(1)}, f32[1024]{0:T(1024)}, u32[]{:S(2)}) %copy-start.14) | copy-done | bytes 4120
  13.0 0.7 %copy-done.15 = s32[1024]{0:T(1024)S(1)} copy-done((s32[1024]{0:T(1024)S(1)}, s32[1024]{0:T(1024)}, u32[]{:S(2)}) %copy-start.15) | copy-done | bytes 4120
  13.7 0.7 %copy-done.17 = s32[16]{0:T(128)S(1)} copy-done((s32[16]{0:T(128)S(1)}, s32[16]{0:T(128)}, u32[]{:S(2)}) %copy-start.17) | copy-done | bytes 88
  14.4 46.1 %shard_map.172 = bf16[32,128]{1,0:T(8,128)(2,1)S(1)} custom-call(bf16[32,1024]{1,0:T(8,128)(2,1)S(1)} %copy-done.9, f32[1,1024]{1,0:T(1,128)S(1)} %bitcast.10, f32[1,1024]{1,0:T(1,128)S(1)} %bitcast.11, s32[16,128]{1,0:T(8,128)S(1)} %bitcast.7, s32[16,128]{1,0:T(8,128)S(1)} %bitcast.8, s32[16,128]{1,0:T(8,128)S(1)} %bitcast.9, s32[1,1024]{1,0:T(1,128)S(1)} %bitcast.12, ...), custom_call_target="tpu_custom_call" | custom-call | tf_op jit(solution)/shard_map/pallas_call | solution.py:368
  60.5 0.6 copy.20
  (6 shorter events, 0.0 us)
Async XLA Ops:
  0.0 0.7 %copy-start.10 = (s32[2048]{0:T(1024)S(1)}, s32[2048]{0:T(1024)}, u32[]{:S(2)}) copy-start(s32[2048]{0:T(1024)} %param.34) | copy-start | bytes 24580
  0.0 0.7 %copy-start.13 = (f32[1024]{0:T(1024)S(1)}, f32[1024]{0:T(1024)}, u32[]{:S(2)}) copy-start(f32[1024]{0:T(1024)} %param.19) | copy-start | bytes 12292
  0.0 0.7 %copy-start.16 = (f32[2,2]{1,0:T(2,128)S(1)}, f32[2,2]{1,0:T(2,128)}, u32[]{:S(2)}) copy-start(f32[2,2]{1,0:T(2,128)} %bias_ref.1) | copy-start | bytes 52
  0.7 1.2 %copy-start = (bf16[1024,512]{1,0:T(8,128)(2,1)S(1)}, bf16[1024,512]{1,0:T(8,128)(2,1)}, u32[]{:S(2)}) copy-start(bf16[1024,512]{1,0:T(8,128)(2,1)} %wg_hbm.1) | copy-start | bytes 3145732
  1.9 1.2 %copy-start.1 = (bf16[1024,512]{1,0:T(8,128)(2,1)S(1)}, bf16[1024,512]{1,0:T(8,128)(2,1)}, u32[]{:S(2)}) copy-start(bf16[1024,512]{1,0:T(8,128)(2,1)} %wu_hbm.1) | copy-start | bytes 3145732
  3.2 1.2 %copy-start.2 = (bf16[512,1024]{1,0:T(8,128)(2,1)S(1)}, bf16[512,1024]{1,0:T(8,128)(2,1)}, u32[]{:S(2)}) copy-start(bf16[512,1024]{1,0:T(8,128)(2,1)} %wd_hbm.1) | copy-start | bytes 3145732
  4.4 0.9 %copy-start.3 = (bf16[1024,128]{1,0:T(8,128)(2,1)S(1)}, bf16[1024,128]{1,0:T(8,128)(2,1)}, u32[]{:S(2)}) copy-start(bf16[1024,128]{1,0:T(8,128)(2,1)} %wq_hbm.1) | copy-start | bytes 786436
  5.3 0.9 %copy-start.4 = (bf16[1024,128]{1,0:T(8,128)(2,1)S(1)}, bf16[1024,128]{1,0:T(8,128)(2,1)}, u32[]{:S(2)}) copy-start(bf16[1024,128]{1,0:T(8,128)(2,1)} %wk_hbm.1) | copy-start | bytes 786436
  6.3 0.9 %copy-start.5 = (bf16[1024,128]{1,0:T(8,128)(2,1)S(1)}, bf16[1024,128]{1,0:T(8,128)(2,1)}, u32[]{:S(2)}) copy-start(bf16[1024,128]{1,0:T(8,128)(2,1)} %wv_hbm.1) | copy-start | bytes 786436
  7.2 0.9 %copy-start.6 = (bf16[1024,128]{1,0:T(8,128)(2,1)S(1)}, bf16[1024,128]{1,0:T(8,128)(2,1)}, u32[]{:S(2)}) copy-start(bf16[1024,128]{1,0:T(8,128)(2,1)} %keys_hbm.1) | copy-start | bytes 786436
  8.2 0.9 %copy-start.7 = (bf16[1024,128]{1,0:T(8,128)(2,1)S(1)}, bf16[1024,128]{1,0:T(8,128)(2,1)}, u32[]{:S(2)}) copy-start(bf16[1024,128]{1,0:T(8,128)(2,1)} %values_hbm.1) | copy-start | bytes 786436
  9.1 0.9 %copy-start.8 = (bf16[128,1024]{1,0:T(8,128)(2,1)S(1)}, bf16[128,1024]{1,0:T(8,128)(2,1)}, u32[]{:S(2)}) copy-start(bf16[128,1024]{1,0:T(8,128)(2,1)} %wo_hbm.1) | copy-start | bytes 786436
  10.1 0.8 %copy-start.9 = (bf16[32,1024]{1,0:T(8,128)(2,1)S(1)}, bf16[32,1024]{1,0:T(8,128)(2,1)}, u32[]{:S(2)}) copy-start(bf16[32,1024]{1,0:T(8,128)(2,1)} %tok_ref.1) | copy-start | bytes 196612
  10.9 0.7 %copy-start.11 = (s32[2048]{0:T(1024)S(1)}, s32[2048]{0:T(1024)}, u32[]{:S(2)}) copy-start(s32[2048]{0:T(1024)} %param.33) | copy-start | bytes 24580
  11.6 0.7 %copy-start.12 = (s32[2048]{0:T(1024)S(1)}, s32[2048]{0:T(1024)}, u32[]{:S(2)}) copy-start(s32[2048]{0:T(1024)} %param.31) | copy-start | bytes 24580
  12.3 0.7 %copy-start.14 = (f32[1024]{0:T(1024)S(1)}, f32[1024]{0:T(1024)}, u32[]{:S(2)}) copy-start(f32[1024]{0:T(1024)} %param.24) | copy-start | bytes 12292
  13.0 0.7 %copy-start.15 = (s32[1024]{0:T(1024)S(1)}, s32[1024]{0:T(1024)}, u32[]{:S(2)}) copy-start(s32[1024]{0:T(1024)} %param.30) | copy-start | bytes 12292
  13.7 0.7 %copy-start.17 = (s32[16]{0:T(128)S(1)}, s32[16]{0:T(128)}, u32[]{:S(2)}) copy-start(s32[16]{0:T(128)} %param.35) | copy-start | bytes 196

commit v2 on v1

--- a/solution.py
+++ b/solution.py
@@ -1,5 +1,3 @@
-import functools
-
 import jax
 import jax.numpy as jnp
 from jax import lax
@@ -37,76 +35,70 @@
     return jnp.dot(a, b, preferred_element_type=F32, precision=HIGH)
 
 
-def kernel(
-    tok_ref,
-    norm_gain_ref,
-    ffn_gain_ref,
-    order_ref,
-    len_ref,
-    query_variate_ref,
-    key_variate_ref,
-    live_ref,
-    bias_ref,
-    wq_hbm,
-    wk_hbm,
-    wv_hbm,
-    keys_hbm,
-    values_hbm,
-    wo_hbm,
-    wg_hbm,
-    wu_hbm,
-    wd_hbm,
-    out_ref,
-    wq,
-    wk,
-    wv,
-    keys,
-    values,
-    wo,
-    wg,
-    wu,
-    wd,
-    q_send,
-    q_recv,
-    p_send,
-    p_recv,
-    c_send,
-    c_recv,
-    d_recv,
-    e_send,
-    e_recv,
-    load_sem,
-    send_sem,
-    recv_sem,
-):
+LOADS = (
+    "order",
+    "lens",
+    "query_variate",
+    "tok",
+    "norm_gain",
+    "wq",
+    "wk",
+    "wv",
+    "key_variate",
+    "live",
+    "keys",
+    "values",
+    "wo",
+    "ffn_gain",
+    "wg",
+    "wu",
+    "wd",
+)
+
+
+def kernel(*refs):
+    n_loads = len(LOADS)
+    bias_ref = refs[0]
+    from_hbm = dict(zip(LOADS, refs[1 : 1 + n_loads]))
+    out_ref = refs[1 + n_loads]
+    at_vmem = dict(zip(LOADS, refs[2 + n_loads : 2 + 2 * n_loads]))
+    (
+        q_send,
+        q_recv,
+        p_send,
+        p_recv,
+        c_send,
+        c_recv,
+        d_recv,
+        e_send,
+        e_recv,
+        load_sem,
+        send_sem,
+        recv_sem,
+    ) = refs[2 + 2 * n_loads :]
     n_blk = q_send.shape[0]
     n_head = c_send.shape[0]
-    reqs, d_model = tok_ref.shape
-    pool = keys.shape[0]
-    n_live = live_ref.shape[1]
+    reqs, d_model = at_vmem["tok"].shape
+    pool = at_vmem["keys"].shape[0]
+    n_live = at_vmem["live"].shape[1]
     block = pool // n_live
     width = c_send.shape[2]
     half = width // 2
     me = lax.axis_index("blk")
     head = lax.axis_index("head")
 
-    loads = []
-    for at, (src, dst) in enumerate(
-        (
-            (wq_hbm, wq),
-            (wk_hbm, wk),
-            (wv_hbm, wv),
-            (keys_hbm, keys),
-            (values_hbm, values),
-            (wo_hbm, wo),
-            (wg_hbm, wg),
-            (wu_hbm, wu),
-            (wd_hbm, wd),
-        )
-    ):
-        copy = pltpu.make_async_copy(src, dst, load_sem.at[at])
-        copy.start()
-        loads.append(copy)
+    copies = {
+        name: pltpu.make_async_copy(from_hbm[name], at_vmem[name], load_sem.at[at])
+        for at, name in enumerate(LOADS)
+    }
+    loaded = set()
+    sent = []
+
+    def need(name):
+        if name not in loaded:
+            loaded.add(name)
+            copies[name].wait()
+        return at_vmem[name]
 
     barrier = pltpu.get_barrier_semaphore()
 
@@ -120,12 +112,14 @@
 
     lax.fori_loop(1, n_blk, greet_blk, 0)
     lax.fori_loop(1, n_head, greet_head, 0)
-
-    order = order_ref[...]
+    for name in LOADS:
+        copies[name].start()
+
+    order = need("order")[...]
     rows, lanes = order.shape
     home = order[0:1, :] >> 5
     local = order & (reqs - 1)
-    packed = (len_ref[...] + (query_variate_ref[...] << 13)).astype(F32)
+    packed = (need("lens")[...] + (need("query_variate")[...] << 13)).astype(F32)
     per_row = lanes // reqs
     table = jnp.zeros((reqs, lanes), F32)
     for part in range(per_row):
@@ -159,11 +153,10 @@
     holds = (end_req > first) & (start_req < first + pool)
     holds_f = holds.astype(F32)
 
-    inputs = tok_ref[...].astype(F32)
+    inputs = need("tok")[...].astype(F32)
     mean_square = jnp.mean(inputs * inputs, axis=1, keepdims=True)
-    normed = (inputs * lax.rsqrt(mean_square + 1e-05) * norm_gain_ref[...]).astype(BF16)
-    loads[0].wait()
-    query = dot(normed, wq[...]).astype(BF16)
+    normed = (inputs * lax.rsqrt(mean_square + 1e-05) * need("norm_gain")[...]).astype(BF16)
+    query = dot(normed, need("wq")[...]).astype(BF16)
     query_f = query.astype(F32)
     routed = dot_tn(holds_f.astype(BF16), query)
     q_send[...] = routed.reshape(n_blk, 1, width)
@@ -184,6 +177,7 @@
             return carry
 
         lax.fori_loop(1, n_blk, step, 0)
+        sent.append((send, at))
 
     def exchange_head(send, recv, at):
         def step(i, carry):
@@ -198,6 +192,7 @@
             return carry
 
         lax.fori_loop(1, n_head, step, 0)
+        sent.append((recv, at))
 
     def wait_bytes(ref, sem, at):
         part = ref.at[pl.ds(0, ref.shape[0] - 1)]
@@ -205,10 +200,8 @@
 
     exchange_blk(q_send, q_recv, 0)
 
-    loads[1].wait()
-    key_new = dot(normed, wk[...]).astype(BF16).astype(F32)
-    loads[2].wait()
-    value_new = dot(normed, wv[...]).astype(BF16).astype(F32)
+    key_new = dot(normed, need("wk")[...]).astype(BF16).astype(F32)
+    value_new = dot(normed, need("wv")[...]).astype(BF16).astype(F32)
     product = query_f * key_new
     left = iota((reqs, width), 1) < half
     scale = 1.0 / (half**0.5)
@@ -226,12 +219,10 @@
     end_slot = jnp.sum(jnp.where(at_home, end_lane, 0.0), axis=1, keepdims=True)
     variate_slot = jnp.sum(jnp.where(at_home, variate_lane, 0.0), axis=1, keepdims=True)
     in_block = (iota((n_live, pool), 1) // block == iota((n_live, pool), 0)).astype(BF16)
-    live = dot(jnp.broadcast_to(live_ref[...].astype(F32).astype(BF16), (8, n_live)), in_block)[0:1, :]
+    live = dot(jnp.broadcast_to(need("live")[...].astype(F32).astype(BF16), (8, n_live)), in_block)[0:1, :]
     token = iota((n_blk, pool), 1).astype(F32)
     mask = (token >= start_slot) & (token < end_slot) & (live > 0.5)
-    same = key_variate_ref[...].astype(F32) == variate_slot
-    loads[3].wait()
-    loads[4].wait()
+    same = need("key_variate")[...].astype(F32) == variate_slot
 
     wait_bytes(q_recv, recv_sem, 0)
     queries = q_recv[...].reshape(n_blk, width)
@@ -239,7 +230,7 @@
     stacked = jnp.concatenate(
         [jnp.where(left_slot, queries, 0.0), jnp.where(left_slot, 0.0, queries)], axis=0
     ).astype(BF16)
-    raw = dot_nt(stacked, keys[...])
+    raw = dot_nt(stacked, need("keys")[...])
     tops, sums, weights = [], [], []
     for at in range(2):
         score = raw[at * n_blk : (at + 1) * n_blk, :] * scale + jnp.where(
@@ -250,7 +241,7 @@
         tops.append(top)
         sums.append(jnp.sum(weight, axis=1, keepdims=True))
         weights.append(weight.astype(BF16))
-    summed = dot(jnp.concatenate(weights, axis=0), values[...])
+    summed = dot(jnp.concatenate(weights, axis=0), need("values")[...])
     summed = jnp.where(left_slot, summed[:n_blk, :], summed[n_blk:, :])
     column = iota((n_blk, width), 1)
     stats = jnp.where(
@@ -285,14 +276,13 @@
         left, own_weight[0], own_weight[1]
     ) * value_new
     attended = (value_final / jnp.where(left, total[0], total[1])).astype(BF16)
-    loads[5].wait()
-    projected = dot(attended, wo[...]).astype(BF16)
+    projected = dot(attended, need("wo")[...]).astype(BF16)
     for at in range(n_head):
         c_send[at] = projected[:, at * width : (at + 1) * width]
     c_recv[pl.ds(head, 1)] = c_send[pl.ds(head, 1)]
     exchange_head(lambda to: c_send.at[to], c_recv, 2)
     wait_bytes(c_recv, recv_sem, 2)
-    mixed = tok_ref[:, pl.ds(pl.multiple_of(head * width, width), width)].astype(F32)
+    mixed = need("tok")[:, pl.ds(pl.multiple_of(head * width, width), width)].astype(F32)
     part = c_recv[0].astype(F32)
     for at in range(1, n_head):
         part = part + c_recv[at].astype(F32)
@@ -309,18 +299,15 @@
     inverse = lax.rsqrt(jnp.sum(square, axis=1, keepdims=True) / d_model + 1e-05)
     hidden_in = jnp.concatenate(
         [
-            (gathered[at] * inverse * ffn_gain_ref[:, at * width : (at + 1) * width]).astype(BF16)
+            (gathered[at] * inverse * need("ffn_gain")[:, at * width : (at + 1) * width]).astype(BF16)
             for at in range(n_head)
         ],
         axis=1,
     )
-    loads[6].wait()
-    gate = dot(hidden_in, wg[...])
-    loads[7].wait()
-    upper_units = dot(hidden_in, wu[...])
+    gate = dot(hidden_in, need("wg")[...])
+    upper_units = dot(hidden_in, need("wu")[...])
     hidden = (gate * jax.nn.sigmoid(gate) * upper_units).astype(BF16)
-    loads[8].wait()
-    down = dot(hidden, wd[...]).astype(BF16)
+    down = dot(hidden, need("wd")[...]).astype(BF16)
     for at in range(n_head):
         e_send[at] = down[:, at * width : (at + 1) * width]
     e_recv[pl.ds(head, 1)] = e_send[pl.ds(head, 1)]
@@ -330,11 +317,8 @@
     for at in range(1, n_head):
         part = part + e_recv[at].astype(F32)
     out_ref[...] = (mixed.astype(F32) + part).astype(BF16)
-    wait_bytes(q_send, send_sem, 0)
-    wait_bytes(p_send, send_sem, 1)
-    wait_bytes(c_send, send_sem, 2)
-    wait_bytes(d_recv, send_sem, 3)
-    wait_bytes(e_send, send_sem, 4)
+    for ref, at in sent:
+        wait_bytes(ref, send_sem, at)
 
 
 def body(
@@ -361,16 +345,33 @@
     n_head = lax.axis_size("head")
     reqs, d_model = tokens.shape
     width = d_model // n_head
-    vmem = pl.BlockSpec(memory_space=pltpu.VMEM)
-    smem = pl.BlockSpec(memory_space=pltpu.SMEM)
-    hbm = pl.BlockSpec(memory_space=pl.ANY)
-    big = (w_query, w_key, w_value, keys, values, w_out, w_gate, w_up, w_down)
+    operands = dict(
+        tok=tokens,
+        norm_gain=norm_gain.reshape(1, -1),
+        ffn_gain=ffn_gain.reshape(1, -1),
+        order=order.reshape(-1, 128),
+        lens=lengths.reshape(-1, 128),
+        query_variate=query_variate.reshape(-1, 128),
+        key_variate=key_variate.reshape(1, -1),
+        live=live_blocks.reshape(1, -1),
+        wq=w_query,
+        wk=w_key,
+        wv=w_value,
+        keys=keys,
+        values=values,
+        wo=w_out,
+        wg=w_gate,
+        wu=w_up,
+        wd=w_down,
+    )
+    loads = [operands[name] for name in LOADS]
     return pl.pallas_call(
         kernel,
         out_shape=jax.ShapeDtypeStruct((reqs, width), BF16),
-        in_specs=[vmem] * 8 + [smem] + [hbm] * len(big),
-        out_specs=vmem,
-        scratch_shapes=[pltpu.VMEM(x.shape, x.dtype) for x in big]
+        in_specs=[pl.BlockSpec(memory_space=pltpu.SMEM)]
+        + [pl.BlockSpec(memory_space=pltpu.HBM)] * len(loads),
+        out_specs=pl.BlockSpec(memory_space=pltpu.VMEM),
+        scratch_shapes=[pltpu.VMEM(x.shape, x.dtype) for x in loads]
         + [
             pltpu.VMEM((n_blk, 1, width), F32),
             pltpu.VMEM((n_blk, 1, width), F32),
@@ -379,25 +380,14 @@
         ]
         + [pltpu.VMEM((n_head, reqs, width), BF16)] * 5
         + [
-            pltpu.SemaphoreType.DMA((len(big),)),
+            pltpu.SemaphoreType.DMA((len(loads),)),
             pltpu.SemaphoreType.DMA((5,)),
             pltpu.SemaphoreType.DMA((5,)),
         ],
         compiler_params=pltpu.CompilerParams(
-            collective_id=0, has_side_effects=True, vmem_limit_bytes=40 * 1024 * 1024
+            collective_id=0, has_side_effects=True, vmem_limit_bytes=56 * 1024 * 1024
         ),
-    )(
-        tokens,
-        norm_gain.reshape(1, -1),
-        ffn_gain.reshape(1, -1),
-        order.reshape(-1, 128),
-        lengths.reshape(-1, 128),
-        query_variate.reshape(-1, 128),
-        key_variate.reshape(1, -1),
-        live_blocks.reshape(1, -1),
-        bias,
-        *big,
-    )
+    )(bias, *loads)
 
 
 def solution(mesh):

time: 61.7 us -> 48.3 us (0.78)
  local copies, waits for them, and re-layouts: 14.9 us -> 1.3 us
  Pallas kernels: 46.1 us -> 46.8 us
    unnamed x37 -> x1, local copies, waits for them, and re-layouts: 14.9 us -> 1.3 us
    pallas_call x1, Pallas kernels: 46.1 us -> 46.8 us  [body(): pl.pallas_call(kernel, out_shape=jax.ShapeDtypeStruct((reqs, width), BF16...]
where the time goes in v2:
time: 48.3 us; the launch traced here: 48.1 us
  Pallas kernels  46.8 us (97%)
  local copies, waits for them, and re-layouts  1.3 us (3%)
    pallas_call x1, Pallas kernels, body(): pl.pallas_call(kernel, out_shape=jax.ShapeDtypeStruct((reqs, width), BF16...  46.8 us
    unnamed x1, local copies, waits for them, and re-layouts  1.3 us

profile of v2, /device:TPU:1, one launch (start us, length us, event | category | flops | bytes accessed | tf_op | source)
XLA Modules:
  0.0 48.1 jit_solution(10249747048851200232)
XLA Ops:
  0.0 46.8 %shard_map.172 = bf16[32,128]{1,0:T(8,128)(2,1)} custom-call(f32[2,2]{1,0:T(2,128)} %refs_0_.1, s32[16,128]{1,0:T(8,128)} %bitcast.7, s32[16,128]{1,0:T(8,128)} %bitcast.8, s32[16,128]{1,0:T(8,128)} %bitcast.9, bf16[32,1024]{1,0:T(8,128)(2,1)} %refs_4_.1, f32[1,1024]{1,0:T(1,128)} %bitcast.10, bf16[1024,128]{1,0:T(8,128)(2,1)} %refs_6_.1, ...), custom_call_target="tpu_custom_call" | custom-call | tf_op jit(solution)/shard_map/pallas_call | solution.py:368
  46.8 1.3 %copy.20 = bf16[32,128]{1,0:T(8,128)(2,1)} copy(bf16[32,128]{1,0:T(8,128)(2,1)} %shard_map.172) | data formatting | bytes 16384

commit v3 on v2

--- a/solution.py
+++ b/solution.py
@@ -9,6 +9,7 @@
 BF16 = jnp.bfloat16
 HIGH = lax.Precision.HIGHEST
 FLOOR = -1e30
+SIDE = 8
 
 
 def iota(shape, dim):
@@ -56,6 +57,33 @@
 )
 
 
+def fold(k):
+    return SIDE // 2 + ((k + 1) // 2) * (1 - 2 * lax.rem(k, 2))
+
+
+def each_blk(me, act):
+    z, y = me // SIDE, lax.rem(me, SIDE)
+    for both in range(2 * SIDE - 2):
+
+        def step(a, carry):
+            to_z = lax.rem(z + fold(a), SIDE)
+            to_y = lax.rem(y + fold(both - a), SIDE)
+            act(to_z * SIDE + to_y)
+            return carry
+
+        lax.fori_loop(max(0, both - SIDE + 1), min(both, SIDE - 1) + 1, step, 0)
+
+
+def each_head(head, n_head, act):
+    chip, core = head // 2, lax.rem(head, 2)
+    chips = n_head // 2
+    for far in (2, 1, 3):
+        to = lax.rem(chip + far, chips) * 2
+        act(to + core)
+        act(to + 1 - core)
+    act(chip * 2 + 1 - core)
+
+
 def kernel(*refs):
     n_loads = len(LOADS)
     bias_ref = refs[0]
@@ -67,26 +95,27 @@
         q_recv,
         p_send,
         p_recv,
-        c_send,
         c_recv,
-        d_recv,
         e_send,
         e_recv,
+        mixed_ref,
         load_sem,
         send_sem,
         recv_sem,
     ) = refs[2 + 2 * n_loads :]
     n_blk = q_send.shape[0]
-    n_head = c_send.shape[0]
+    n_head = c_recv.shape[0]
     reqs, d_model = at_vmem["tok"].shape
     pool = at_vmem["keys"].shape[0]
     n_live = at_vmem["live"].shape[1]
     block = pool // n_live
-    width = c_send.shape[2]
+    width = c_recv.shape[2]
     half = width // 2
     me = lax.axis_index("blk")
     head = lax.axis_index("head")
 
+    wo_all = at_vmem["wo"]
+    at_vmem["wo"] = wo_all.at[head]
     copies = {
         name: pltpu.make_async_copy(from_hbm[name], at_vmem[name], load_sem.at[at])
         for at, name in enumerate(LOADS)
@@ -102,16 +131,10 @@
 
     barrier = pltpu.get_barrier_semaphore()
 
-    def greet_blk(i, carry):
-        pl.semaphore_signal(barrier, inc=1, device_id={"blk": lax.rem(me + i, n_blk)})
-        return carry
-
-    def greet_head(i, carry):
-        pl.semaphore_signal(barrier, inc=1, device_id={"head": lax.rem(head + i, n_head)})
-        return carry
-
-    lax.fori_loop(1, n_blk, greet_blk, 0)
-    lax.fori_loop(1, n_head, greet_head, 0)
+    each_blk(me, lambda to: pl.semaphore_signal(barrier, inc=1, device_id={"blk": to}))
+    each_head(
+        head, n_head, lambda to: pl.semaphore_signal(barrier, inc=1, device_id={"head": to})
+    )
     for name in LOADS:
         copies[name].start()
 
@@ -165,8 +188,7 @@
     pl.semaphore_wait(barrier, n_blk + n_head - 2)
 
     def exchange_blk(send, recv, at):
-        def step(i, carry):
-            to = lax.rem(me + i, n_blk)
+        def start(to):
             pltpu.make_async_remote_copy(
                 src_ref=send.at[to],
                 dst_ref=recv.at[me],
@@ -174,14 +196,12 @@
                 recv_sem=recv_sem.at[at],
                 device_id={"blk": to},
             ).start()
-            return carry
-
-        lax.fori_loop(1, n_blk, step, 0)
-        sent.append((send, at))
+
+        each_blk(me, start)
+        sent.append((send, n_blk - 1, at))
 
     def exchange_head(send, recv, at):
-        def step(i, carry):
-            to = lax.rem(head + i, n_head)
+        def start(to):
             pltpu.make_async_remote_copy(
                 src_ref=send(to),
                 dst_ref=recv.at[head],
@@ -189,16 +209,32 @@
                 recv_sem=recv_sem.at[at],
                 device_id={"head": to},
             ).start()
-            return carry
-
-        lax.fori_loop(1, n_head, step, 0)
-        sent.append((recv, at))
-
-    def wait_bytes(ref, sem, at):
-        part = ref.at[pl.ds(0, ref.shape[0] - 1)]
+
+        each_head(head, n_head, start)
+        sent.append((recv, n_head - 1, at))
+
+    def share(src, slot, to, at):
+        pltpu.make_async_remote_copy(
+            src_ref=src,
+            dst_ref=wo_all.at[slot],
+            send_sem=send_sem.at[at],
+            recv_sem=recv_sem.at[at],
+            device_id={"head": to},
+        ).start()
+
+    def wait_bytes(ref, count, sem, at):
+        part = ref.at[pl.ds(0, count)]
         pltpu.make_async_copy(part, part, sem.at[at]).wait()
 
     exchange_blk(q_send, q_recv, 0)
+
+    chips = n_head // 2
+    sibling = (head // 2) * 2 + 1 - lax.rem(head, 2)
+    for far in (2, 1, 3):
+        share(from_hbm["wo"], head, lax.rem(head + 2 * far, n_head), 4)
+    share(from_hbm["wo"], head, sibling, 5)
+    sent.append((wo_all, chips - 1, 4))
+    sent.append((wo_all, chips, 5))
 
     key_new = dot(normed, need("wk")[...]).astype(BF16).astype(F32)
     value_new = dot(normed, need("wv")[...]).astype(BF16).astype(F32)
@@ -224,7 +260,7 @@
     mask = (token >= start_slot) & (token < end_slot) & (live > 0.5)
     same = need("key_variate")[...].astype(F32) == variate_slot
 
-    wait_bytes(q_recv, recv_sem, 0)
+    wait_bytes(q_recv, n_blk - 1, recv_sem, 0)
     queries = q_recv[...].reshape(n_blk, width)
     left_slot = iota((n_blk, width), 1) < half
     stacked = jnp.concatenate(
@@ -253,7 +289,11 @@
     p_send[:, 1:2, :] = stats.reshape(n_blk, 1, width)
     p_recv[pl.ds(me, 1)] = p_send[pl.ds(me, 1)]
     exchange_blk(p_send, p_recv, 1)
-    wait_bytes(p_recv, recv_sem, 1)
+    wait_bytes(wo_all, chips - 1, recv_sem, 4)
+    for far in (2, 1, 3):
+        slot = lax.rem(head + 2 * far, n_head)
+        share(wo_all.at[slot], slot, sibling, 5)
+    wait_bytes(p_recv, n_blk - 1, recv_sem, 1)
 
     part_sum = p_recv[:, 0:1, :].reshape(n_blk, width)
     part_stat = p_recv[:, 1:2, :].reshape(n_blk, width)
@@ -276,34 +316,18 @@
         left, own_weight[0], own_weight[1]
     ) * value_new
     attended = (value_final / jnp.where(left, total[0], total[1])).astype(BF16)
-    projected = dot(attended, need("wo")[...]).astype(BF16)
+    c_recv[pl.ds(head, 1)] = attended.reshape(1, reqs, width)
+    exchange_head(lambda to: c_recv.at[head], c_recv, 2)
+    wait_bytes(wo_all, chips, recv_sem, 5)
+    need("wo")
+    wait_bytes(c_recv, n_head - 1, recv_sem, 2)
+    attended_all = jnp.concatenate([c_recv[at] for at in range(n_head)], axis=1)
+    projected = dot(attended_all, wo_all[...].reshape(d_model, d_model))
+    mixed = (inputs + projected).astype(BF16).astype(F32)
     for at in range(n_head):
-        c_send[at] = projected[:, at * width : (at + 1) * width]
-    c_recv[pl.ds(head, 1)] = c_send[pl.ds(head, 1)]
-    exchange_head(lambda to: c_send.at[to], c_recv, 2)
-    wait_bytes(c_recv, recv_sem, 2)
-    mixed = need("tok")[:, pl.ds(pl.multiple_of(head * width, width), width)].astype(F32)
-    part = c_recv[0].astype(F32)
-    for at in range(1, n_head):
-        part = part + c_recv[at].astype(F32)
-    mixed = (mixed + part).astype(BF16)
-    d_recv[pl.ds(head, 1)] = mixed.reshape(1, reqs, width)
-    exchange_head(lambda to: d_recv.at[head], d_recv, 3)
-    wait_bytes(d_recv, recv_sem, 3)
-    square = jnp.zeros((reqs, width), F32)
-    gathered = []
-    for at in range(n_head):
-        piece = d_recv[at].astype(F32)
-        gathered.append(piece)
-        square = square + piece * piece
-    inverse = lax.rsqrt(jnp.sum(square, axis=1, keepdims=True) / d_model + 1e-05)
-    hidden_in = jnp.concatenate(
-        [
-            (gathered[at] * inverse * need("ffn_gain")[:, at * width : (at + 1) * width]).astype(BF16)
-            for at in range(n_head)
-        ],
-        axis=1,
-    )
+        mixed_ref[at] = mixed[:, at * width : (at + 1) * width]
+    inverse = lax.rsqrt(jnp.mean(mixed * mixed, axis=1, keepdims=True) + 1e-05)
+    hidden_in = (mixed * inverse * need("ffn_gain")[...]).astype(BF16)
     gate = dot(hidden_in, need("wg")[...])
     upper_units = dot(hidden_in, need("wu")[...])
     hidden = (gate * jax.nn.sigmoid(gate) * upper_units).astype(BF16)
@@ -311,14 +335,14 @@
     for at in range(n_head):
         e_send[at] = down[:, at * width : (at + 1) * width]
     e_recv[pl.ds(head, 1)] = e_send[pl.ds(head, 1)]
-    exchange_head(lambda to: e_send.at[to], e_recv, 4)
-    wait_bytes(e_recv, recv_sem, 4)
+    exchange_head(lambda to: e_send.at[to], e_recv, 3)
+    wait_bytes(e_recv, n_head - 1, recv_sem, 3)
     part = e_recv[0].astype(F32)
     for at in range(1, n_head):
         part = part + e_recv[at].astype(F32)
-    out_ref[...] = (mixed.astype(F32) + part).astype(BF16)
-    for ref, at in sent:
-        wait_bytes(ref, send_sem, at)
+    out_ref[...] = (mixed_ref[head] + part).astype(BF16)
+    for ref, count, at in sent:
+        wait_bytes(ref, count, send_sem, at)
 
 
 def body(
@@ -371,18 +395,22 @@
         in_specs=[pl.BlockSpec(memory_space=pltpu.SMEM)]
         + [pl.BlockSpec(memory_space=pltpu.HBM)] * len(loads),
         out_specs=pl.BlockSpec(memory_space=pltpu.VMEM),
-        scratch_shapes=[pltpu.VMEM(x.shape, x.dtype) for x in loads]
+        scratch_shapes=[
+            pltpu.VMEM((n_head,) * (name == "wo") + x.shape, x.dtype)
+            for name, x in zip(LOADS, loads)
+        ]
         + [
             pltpu.VMEM((n_blk, 1, width), F32),
             pltpu.VMEM((n_blk, 1, width), F32),
             pltpu.VMEM((n_blk, 2, width), F32),
             pltpu.VMEM((n_blk, 2, width), F32),
         ]
-        + [pltpu.VMEM((n_head, reqs, width), BF16)] * 5
+        + [pltpu.VMEM((n_head, reqs, width), BF16)] * 3
+        + [pltpu.VMEM((n_head, reqs, width), F32)]
         + [
             pltpu.SemaphoreType.DMA((len(loads),)),
-            pltpu.SemaphoreType.DMA((5,)),
-            pltpu.SemaphoreType.DMA((5,)),
+            pltpu.SemaphoreType.DMA((6,)),
+            pltpu.SemaphoreType.DMA((6,)),
         ],
         compiler_params=pltpu.CompilerParams(
             collective_id=0, has_side_effects=True, vmem_limit_bytes=56 * 1024 * 1024

time: 48.3 us -> 44.5 us (0.921)
  Pallas kernels: 46.8 us -> 42.9 us
    pallas_call x1, Pallas kernels: 46.8 us -> 42.9 us  [body(): pl.pallas_call(kernel, out_shape=jax.ShapeDtypeStruct((reqs, width), BF16...]
where the time goes in v3:
time: 44.5 us; the launch traced here: 44.2 us
  Pallas kernels  42.9 us (96%)
  local copies, waits for them, and re-layouts  1.3 us (3%)
    pallas_call x1, Pallas kernels, body(): pl.pallas_call(kernel, out_shape=jax.ShapeDtypeStruct((reqs, width), BF16...  42.9 us
    unnamed x1, local copies, waits for them, and re-layouts  1.3 us

profile of v3, /device:TPU:1, one launch (start us, length us, event | category | flops | bytes accessed | tf_op | source)
XLA Modules:
  0.0 44.2 jit_solution(8548684782241884829)
XLA Ops:
  0.0 42.9 %shard_map.172 = bf16[32,128]{1,0:T(8,128)(2,1)} custom-call(f32[2,2]{1,0:T(2,128)} %refs_0_.1, s32[16,128]{1,0:T(8,128)} %bitcast.7, s32[16,128]{1,0:T(8,128)} %bitcast.8, s32[16,128]{1,0:T(8,128)} %bitcast.9, bf16[32,1024]{1,0:T(8,128)(2,1)} %refs_4_.1, f32[1,1024]{1,0:T(1,128)} %bitcast.10, bf16[1024,128]{1,0:T(8,128)(2,1)} %refs_6_.1, ...), custom_call_target="tpu_custom_call" | custom-call | tf_op jit(solution)/shard_map/pallas_call | solution.py:392
  42.9 1.3 %copy.20 = bf16[32,128]{1,0:T(8,128)(2,1)} copy(bf16[32,128]{1,0:T(8,128)(2,1)} %shard_map.172) | data formatting | bytes 16384

commit v4 on v3

--- a/solution.py
+++ b/solution.py
@@ -10,6 +10,7 @@
 HIGH = lax.Precision.HIGHEST
 FLOOR = -1e30
 SIDE = 8
+EARLY = 6
 
 
 def iota(shape, dim):
@@ -57,31 +58,28 @@
 )
 
 
-def fold(k):
-    return SIDE // 2 + ((k + 1) // 2) * (1 - 2 * lax.rem(k, 2))
+def ring(k):
+    return min(k, SIDE - k)
+
+
+FAR_FIRST = sorted(
+    ((dz, dy) for dz in range(SIDE) for dy in range(SIDE) if dz or dy),
+    key=lambda step: -ring(step[0]) - ring(step[1]),
+)
 
 
 def each_blk(me, act):
-    z, y = me // SIDE, lax.rem(me, SIDE)
-    for both in range(2 * SIDE - 2):
-
-        def step(a, carry):
-            to_z = lax.rem(z + fold(a), SIDE)
-            to_y = lax.rem(y + fold(both - a), SIDE)
-            act(to_z * SIDE + to_y)
-            return carry
-
-        lax.fori_loop(max(0, both - SIDE + 1), min(both, SIDE - 1) + 1, step, 0)
+    low = SIDE - 1
+    for dz, dy in FAR_FIRST:
+        act(((me + SIDE * dz) & (SIDE * low)) | ((me + dy) & low))
 
 
 def each_head(head, n_head, act):
-    chip, core = head // 2, lax.rem(head, 2)
-    chips = n_head // 2
     for far in (2, 1, 3):
-        to = lax.rem(chip + far, chips) * 2
-        act(to + core)
-        act(to + 1 - core)
-    act(chip * 2 + 1 - core)
+        to = (head + 2 * far) & (n_head - 1)
+        act(to)
+        act(to ^ 1)
+    act(head ^ 1)
 
 
 def kernel(*refs):
@@ -111,6 +109,7 @@
     block = pool // n_live
     width = c_recv.shape[2]
     half = width // 2
+    scale = 1.0 / (half**0.5)
     me = lax.axis_index("blk")
     head = lax.axis_index("head")
 
@@ -131,11 +130,13 @@
 
     barrier = pltpu.get_barrier_semaphore()
 
+    for name in LOADS[:EARLY]:
+        copies[name].start()
     each_blk(me, lambda to: pl.semaphore_signal(barrier, inc=1, device_id={"blk": to}))
     each_head(
         head, n_head, lambda to: pl.semaphore_signal(barrier, inc=1, device_id={"head": to})
     )
-    for name in LOADS:
+    for name in LOADS[EARLY:]:
         copies[name].start()
 
     order = need("order")[...]
@@ -181,7 +182,7 @@
     normed = (inputs * lax.rsqrt(mean_square + 1e-05) * need("norm_gain")[...]).astype(BF16)
     query = dot(normed, need("wq")[...]).astype(BF16)
     query_f = query.astype(F32)
-    routed = dot_tn(holds_f.astype(BF16), query)
+    routed = dot_tn(holds_f.astype(BF16), query) * scale
     q_send[...] = routed.reshape(n_blk, 1, width)
     q_recv[pl.ds(me, 1)] = q_send[pl.ds(me, 1)]
 
@@ -229,9 +230,9 @@
     exchange_blk(q_send, q_recv, 0)
 
     chips = n_head // 2
-    sibling = (head // 2) * 2 + 1 - lax.rem(head, 2)
+    sibling = head ^ 1
     for far in (2, 1, 3):
-        share(from_hbm["wo"], head, lax.rem(head + 2 * far, n_head), 4)
+        share(from_hbm["wo"], head, (head + 2 * far) & (n_head - 1), 4)
     share(from_hbm["wo"], head, sibling, 5)
     sent.append((wo_all, chips - 1, 4))
     sent.append((wo_all, chips, 5))
@@ -240,7 +241,6 @@
     value_new = dot(normed, need("wv")[...]).astype(BF16).astype(F32)
     product = query_f * key_new
     left = iota((reqs, width), 1) < half
-    scale = 1.0 / (half**0.5)
     own = [
         jnp.sum(jnp.where(left, product, 0.0), axis=1, keepdims=True) * scale + bias_ref[0, 0],
         jnp.sum(jnp.where(left, 0.0, product), axis=1, keepdims=True) * scale + bias_ref[0, 1],
@@ -260,6 +260,10 @@
     mask = (token >= start_slot) & (token < end_slot) & (live > 0.5)
     same = need("key_variate")[...].astype(F32) == variate_slot
 
+    shift = [
+        jnp.where(mask, jnp.where(same, bias_ref[0, at], bias_ref[1, at]), FLOOR)
+        for at in range(2)
+    ]
     wait_bytes(q_recv, n_blk - 1, recv_sem, 0)
     queries = q_recv[...].reshape(n_blk, width)
     left_slot = iota((n_blk, width), 1) < half
@@ -269,11 +273,9 @@
     raw = dot_nt(stacked, need("keys")[...])
     tops, sums, weights = [], [], []
     for at in range(2):
-        score = raw[at * n_blk : (at + 1) * n_blk, :] * scale + jnp.where(
-            same, bias_ref[0, at], bias_ref[1, at]
-        )
-        top = jnp.max(jnp.where(mask, score, FLOOR), axis=1, keepdims=True)
-        weight = jnp.where(mask, jnp.exp(score - top), 0.0)
+        score = raw[at * n_blk : (at + 1) * n_blk, :] + shift[at]
+        top = jnp.max(score, axis=1, keepdims=True)
+        weight = jnp.exp(score - top)
         tops.append(top)
         sums.append(jnp.sum(weight, axis=1, keepdims=True))
         weights.append(weight.astype(BF16))
@@ -291,7 +293,7 @@
     exchange_blk(p_send, p_recv, 1)
     wait_bytes(wo_all, chips - 1, recv_sem, 4)
     for far in (2, 1, 3):
-        slot = lax.rem(head + 2 * far, n_head)
+        slot = (head + 2 * far) & (n_head - 1)
         share(wo_all.at[slot], slot, sibling, 5)
     wait_bytes(p_recv, n_blk - 1, recv_sem, 1)
 

time: 44.5 us -> 43.5 us (0.978)
  Pallas kernels: 42.9 us -> 41.9 us
    pallas_call x1, Pallas kernels: 42.9 us -> 41.9 us  [body(): pl.pallas_call(kernel, out_shape=jax.ShapeDtypeStruct((reqs, width), BF16...]
where the time goes in v4:
time: 43.5 us; the launch traced here: 43.2 us
  Pallas kernels  41.9 us (96%)
  local copies, waits for them, and re-layouts  1.3 us (3%)
    pallas_call x1, Pallas kernels, body(): pl.pallas_call(kernel, out_shape=jax.ShapeDtypeStruct((reqs, width), BF16...  41.9 us
    unnamed x1, local copies, waits for them, and re-layouts  1.3 us

profile of v4, /device:TPU:1, one launch (start us, length us, event | category | flops | bytes accessed | tf_op | source)
XLA Modules:
  0.0 43.2 jit_solution(16881969772962324412)
XLA Ops:
  0.0 41.9 %shard_map.172 = bf16[32,128]{1,0:T(8,128)(2,1)} custom-call(f32[2,2]{1,0:T(2,128)} %refs_0_.1, s32[16,128]{1,0:T(8,128)} %bitcast.7, s32[16,128]{1,0:T(8,128)} %bitcast.8, s32[16,128]{1,0:T(8,128)} %bitcast.9, bf16[32,1024]{1,0:T(8,128)(2,1)} %refs_4_.1, f32[1,1024]{1,0:T(1,128)} %bitcast.10, bf16[1024,128]{1,0:T(8,128)(2,1)} %refs_6_.1, ...), custom_call_target="tpu_custom_call" | custom-call | tf_op jit(solution)/shard_map/pallas_call | solution.py:394
  41.9 1.3 %copy.20 = bf16[32,128]{1,0:T(8,128)(2,1)} copy(bf16[32,128]{1,0:T(8,128)(2,1)} %shard_map.172) | data formatting | bytes 16384

commit v5 on v4

--- a/solution.py
+++ b/solution.py
@@ -136,31 +136,43 @@
     each_head(
         head, n_head, lambda to: pl.semaphore_signal(barrier, inc=1, device_id={"head": to})
     )
-    for name in LOADS[EARLY:]:
-        copies[name].start()
 
     order = need("order")[...]
     rows, lanes = order.shape
     home = order[0:1, :] >> 5
     local = order & (reqs - 1)
-    packed = (need("lens")[...] + (need("query_variate")[...] << 13)).astype(F32)
+    lens = need("lens")[...]
+    coarse = (lens >> 6).astype(F32)
+    fine = ((lens & 63) + (need("query_variate")[...] << 6)).astype(F32)
+    both = jnp.concatenate([coarse, fine], axis=1).astype(BF16)
     per_row = lanes // reqs
+    pick = jnp.concatenate(
+        [
+            (home == iota((rows, lanes), 0) * per_row + part).astype(F32)
+            for part in range(per_row)
+        ],
+        axis=1,
+    ).astype(BF16)
+    found = dot_tn(both, pick)
+    found = 256.0 * found[:lanes, :] + found[lanes:, :]
     table = jnp.zeros((reqs, lanes), F32)
     for part in range(per_row):
-        pick = (home == iota((rows, lanes), 0) * per_row + part).astype(F32)
-        found = dot_tn(packed, pick, HIGH)
-        table = table + found[part * reqs : (part + 1) * reqs, :]
-    ordered = jnp.zeros((rows, lanes), F32)
-    for slot in range(reqs):
-        ordered = ordered + jnp.where(local == slot, table[slot : slot + 1, :], 0.0)
-    ordered = ordered.astype(jnp.int32)
-    variate = (ordered >> 13).astype(F32)
-    length = (ordered & 8191).astype(F32)
-    upper = (iota((lanes, lanes), 0) <= iota((lanes, lanes), 1)).astype(F32)
-    prefix = row_dot(length, upper)
-    below = (iota((rows, rows), 1) < iota((rows, rows), 0)).astype(F32)
-    totals = jnp.broadcast_to(jnp.sum(length, axis=1, keepdims=True), (rows, lanes))
-    ends = prefix + row_dot(below, totals)
+        at_row, at_lane = part * reqs, part * lanes
+        table = table + found[at_row : at_row + reqs, at_lane : at_lane + lanes]
+    picked = [jnp.where(local == slot, table[slot : slot + 1, :], 0.0) for slot in range(reqs)]
+    while len(picked) > 1:
+        picked = [a + b for a, b in zip(picked[::2], picked[1::2])]
+    ordered = picked[0].astype(jnp.int32)
+    variate = ((ordered >> 6) & 3).astype(F32)
+    coarse = (ordered >> 8).astype(F32)
+    fine = (ordered & 63).astype(F32)
+    length = 64.0 * coarse + fine
+    upper = (iota((lanes, lanes), 0) <= iota((lanes, lanes), 1)).astype(F32).astype(BF16)
+    prefix = dot(jnp.concatenate([coarse, fine], axis=0).astype(BF16), upper)
+    below = (iota((rows, rows), 1) < iota((rows, rows), 0)).astype(F32).astype(BF16)
+    above = dot(below, jnp.concatenate([coarse, fine], axis=1).astype(BF16))
+    above = jnp.sum(64.0 * above[:, :lanes] + above[:, lanes:], axis=1, keepdims=True)
+    ends = 64.0 * prefix[:rows, :] + prefix[rows:, :] + above
     starts = ends - length
 
     mine = jnp.where(home == me, local, -1)
@@ -228,6 +240,9 @@
         pltpu.make_async_copy(part, part, sem.at[at]).wait()
 
     exchange_blk(q_send, q_recv, 0)
+
+    for name in LOADS[EARLY:]:
+        copies[name].start()
 
     chips = n_head // 2
     sibling = head ^ 1
@@ -301,7 +316,7 @@
     part_stat = p_recv[:, 1:2, :].reshape(n_blk, width)
     choose = (iota((8, width), 0) == iota((8, width), 1)).astype(F32)
     by_lane = dot_nt(choose, part_stat, HIGH)
-    merged, total = [], []
+    factors, total = [], []
     own_weight = []
     for at in range(2):
         part_top = by_lane[at : at + 1, :]
@@ -313,8 +328,17 @@
         mine_weight = jnp.exp(own[at] - top)
         total.append(jnp.sum(factor * part_total, axis=1, keepdims=True) + mine_weight)
         own_weight.append(mine_weight)
-        merged.append(row_dot(factor, part_sum))
-    value_final = jnp.where(left, merged[0], merged[1]) + jnp.where(
+        factors.append(factor)
+    factor = jnp.concatenate(factors, axis=0)
+    factor_high = factor.astype(BF16)
+    factor_low = (factor - factor_high.astype(F32)).astype(BF16)
+    sum_high = part_sum.astype(BF16)
+    sum_low = (part_sum - sum_high.astype(F32)).astype(BF16)
+    merged = dot(
+        jnp.concatenate([factor_high, factor_low], axis=1),
+        jnp.concatenate([sum_high, sum_high], axis=0),
+    ) + dot(factor_high, sum_low)
+    value_final = jnp.where(left, merged[:reqs, :], merged[reqs:, :]) + jnp.where(
         left, own_weight[0], own_weight[1]
     ) * value_new
     attended = (value_final / jnp.where(left, total[0], total[1])).astype(BF16)

time: 43.5 us -> 43.4 us (level)
  no operation moved by 1% of the time
where the time goes in v5:
time: 43.4 us; the launch traced here: 43.2 us
  Pallas kernels  41.9 us (97%)
  local copies, waits for them, and re-layouts  1.3 us (3%)
    pallas_call x1, Pallas kernels, body(): pl.pallas_call(kernel, out_shape=jax.ShapeDtypeStruct((reqs, width), BF16...  41.9 us
    unnamed x1, local copies, waits for them, and re-layouts  1.3 us

profile of v5, /device:TPU:1, one launch (start us, length us, event | category | flops | bytes accessed | tf_op | source)
XLA Modules:
  0.0 43.2 jit_solution(960206536686999300)
XLA Ops:
  0.0 41.9 %shard_map.172 = bf16[32,128]{1,0:T(8,128)(2,1)} custom-call(f32[2,2]{1,0:T(2,128)} %refs_0_.1, s32[16,128]{1,0:T(8,128)} %bitcast.7, s32[16,128]{1,0:T(8,128)} %bitcast.8, s32[16,128]{1,0:T(8,128)} %bitcast.9, bf16[32,1024]{1,0:T(8,128)(2,1)} %refs_4_.1, f32[1,1024]{1,0:T(1,128)} %bitcast.10, bf16[1024,128]{1,0:T(8,128)(2,1)} %refs_6_.1, ...), custom_call_target="tpu_custom_call" | custom-call | tf_op jit(solution)/shard_map/pallas_call | solution.py:418
  41.9 1.3 %copy.20 = bf16[32,128]{1,0:T(8,128)(2,1)} copy(bf16[32,128]{1,0:T(8,128)(2,1)} %shard_map.172) | data formatting | bytes 16384
